TPU v7x, 512 devices: a whole 4x4x16 slice. The times are simulated.
512 devices in a mesh: head: 8 (over y, core), seq: 64 (over z, x).
Axes of the slice: x: 4, y: 4, z: 16, core: 2. Of those that a mesh axis runs over, the one named last changes fastest.
Arguments:
- queries: bfloat16 [16384, 4096], P('seq', 'head'), may hold values from -6 to 6
- keys: bfloat16 [16384, 4096], P('seq', 'head'), may hold values from -6 to 6
- values: bfloat16 [16384, 4096], P('seq', 'head'), may hold values from -6 to 6
- token_rates: float32 [16, 16384], P('head', 'seq'), may hold values from 0.05 to 1
- w_gate: bfloat16 [16, 256, 512], P('head'), may hold values from -6 to 6
- w_up: bfloat16 [16, 256, 512], P('head'), may hold values from -6 to 6
- w_down: bfloat16 [16, 512, 256], P('head'), may hold values from -6 to 6
Outputs:
- applied: bfloat16 [16384, 4096], P('seq', 'head')
- step_gate: bfloat16 [16, 256, 512], P('head')
- step_up: bfloat16 [16, 256, 512], P('head')
- step_down: bfloat16 [16, 256, 512], P('head')
All inputs are finite; a program needn't handle non-finite values.
Results may differ from a plain program's by a relative error of at most 0.035.
Values may be sent and summed in bfloat16 or wider, within the bound.
A program may use at most 64 MiB of HBM per device.

v0:
```python
import math

import jax
import jax.numpy as jnp
from jax import lax
from jax.sharding import PartitionSpec as P

NS_STEPS = 5


def newton_batch(xmat, width):
    for step in range(NS_STEPS):
        amat = jnp.einsum("mdf,mef->mde", xmat, xmat, preferred_element_type=jnp.float32).astype(
            jnp.bfloat16
        )
        square = jnp.einsum("mde,mef->mdf", amat, amat, preferred_element_type=jnp.float32)
        bmat = (-4.775 * amat.astype(jnp.float32) + 2.0315 * square).astype(jnp.bfloat16)
        nxt = 3.4445 * xmat.astype(jnp.float32) + jnp.einsum(
            "mde,mef->mdf", bmat, xmat, preferred_element_type=jnp.float32
        )
        if step == NS_STEPS - 1:
            nxt = nxt * (0.2 * math.sqrt(width))
        xmat = nxt.astype(jnp.bfloat16)
    return xmat


def per_device(queries, keys, values, token_rates, w_gate, w_up, w_down):
    head_count, head_size, hidden = w_gate.shape
    tokens = queries.shape[0]
    scale_one = head_size ** (-0.5)
    scale_two = hidden ** (-0.5)
    qpart = queries.reshape(tokens, head_count, head_size)
    kpart = keys.reshape(tokens, head_count, head_size)
    vpart = values.reshape(tokens, head_count, head_size)
    gq = scale_one * jnp.einsum("thd,hdf->htf", qpart, w_gate, preferred_element_type=jnp.float32)
    uq = scale_one * jnp.einsum("thd,hdf->htf", qpart, w_up, preferred_element_type=jnp.float32)
    hq = (jax.nn.silu(gq) * uq).astype(jnp.bfloat16)
    applied = (
        scale_two * jnp.einsum("htf,hfd->thd", hq, w_down, preferred_element_type=jnp.float32)
    ).astype(jnp.bfloat16)
    applied = applied.reshape(tokens, head_count * head_size)
    gk = scale_one * jnp.einsum("thd,hdf->htf", kpart, w_gate, preferred_element_type=jnp.float32)
    uk = scale_one * jnp.einsum("thd,hdf->htf", kpart, w_up, preferred_element_type=jnp.float32)
    hk = (jax.nn.silu(gk) * uk).astype(jnp.bfloat16)
    vrate = (jnp.transpose(token_rates)[:, :, None] * vpart.astype(jnp.float32)).astype(
        jnp.bfloat16
    )
    gdown = -scale_two * jnp.einsum("thd,htf->hdf", vrate, hk, preferred_element_type=jnp.float32)
    dhid = -scale_two * jnp.einsum(
        "thd,hfd->htf", vrate, w_down, preferred_element_type=jnp.float32
    )
    sig = jax.nn.sigmoid(gk)
    dgate = (dhid * uk * sig * (1.0 + gk * (1.0 - sig))).astype(jnp.bfloat16)
    dup = (dhid * jax.nn.silu(gk)).astype(jnp.bfloat16)
    ggate = scale_one * jnp.einsum("thd,htf->hdf", kpart, dgate, preferred_element_type=jnp.float32)
    gup = scale_one * jnp.einsum("thd,htf->hdf", kpart, dup, preferred_element_type=jnp.float32)
    stacked = jnp.stack([ggate, gup, gdown], axis=1)
    total = lax.psum(stacked, "seq")
    norms = jnp.sqrt(jnp.sum(total * total, axis=(2, 3)))
    xmat = (total / (norms[:, :, None, None] + 1e-07)).astype(jnp.bfloat16)
    result = newton_batch(xmat.reshape(head_count * 3, head_size, hidden), hidden)
    result = result.reshape(head_count, 3, head_size, hidden)
    return (applied, result[:, 0], result[:, 1], result[:, 2])


def solution(mesh):
    in_specs = (
        P("seq", "head"),
        P("seq", "head"),
        P("seq", "head"),
        P("head", "seq"),
        P("head", None, None),
        P("head", None, None),
        P("head", None, None),
    )
    out_specs = (
        P("seq", "head"),
        P("head", None, None),
        P("head", None, None),
        P("head", None, None),
    )
    return jax.shard_map(
        per_device, mesh=mesh, in_specs=in_specs, out_specs=out_specs, check_vma=False
    )
```

profile of v0, /device:TPU:24, one launch (start us, length us, event | category | flops | bytes accessed | tf_op | source)
XLA Modules:
  0.0 338.0 jit_solution(10176853646496948407)
XLA Ops:
  7.2 0.0 copy-start
  7.2 0.0 copy-start.6
  7.2 0.0 copy-start.8
  7.2 0.0 all-reduce.2.cloned.1.call-start
  7.2 1.2 copy.50
  8.4 0.0 copy-done
  8.4 0.0 copy-start.7
  8.4 0.0 copy-start.10
  8.5 1.3 convolution_multiply_fusion.3
  9.8 0.0 copy-done.6
  9.8 0.0 copy-done.8
  9.8 0.3 convolution_multiply_fusion.4
  10.1 0.0 copy-done.7
  10.1 0.0 copy-done.10
  10.1 0.3 convolution_multiply_fusion.5
  10.5 0.5 fusion
  11.0 0.7 fusion.2
  11.7 0.5 fusion.1
  12.2 2.0 pad_maximum_fusion
  14.2 0.0 copy-start.9
  14.2 0.0 all-reduce.2.cloned.1.call-update
  14.2 0.9 copy-done.9
  15.2 0.3 convolution_multiply_fusion.7
  15.5 0.7 fusion.7
  16.2 0.8 copy.43
  17.0 286.8 %all-reduce.2.cloned.1.call-done = f32[2,3,256,512]{3,2,0,1:T(8,128)} async-done(((f32[2,3,256,512]{3,2,0,1:T(8,128)}), f32[2,3,256,512]{3,2,0,1:T(8,128)}) %all-reduce.2.cloned.1.call-update) | async-done | bytes 3145744 | tf_op jit(solution)/shard_map/psum | solution.py:58
  303.8 0.0 copy-start.1
  303.8 2.4 multiply_reduce_fusion
  306.2 0.4 copy-done.1
  306.6 0.5 divide_convert_fusion
  307.1 0.2 copy.39
  307.3 0.6 convolution_convert_fusion.4
  307.9 2.0 add_convert_fusion.3
  309.9 0.0 copy-start.2
  309.9 2.6 convolution_convert_fusion.3
  312.5 0.0 copy-done.2
  312.6 2.0 add_convert_fusion.2
  314.6 0.0 copy-start.3
  314.6 2.6 convolution_convert_fusion.2
  317.2 0.0 copy-done.3
  317.2 2.0 add_convert_fusion.1
  319.2 2.6 convolution_convert_fusion.1
  321.8 0.0 copy-done.4
  321.8 2.0 add_convert_fusion
  323.8 2.6 convolution_convert_fusion
  326.4 0.0 copy-done.5
  326.5 2.2 multiply_convert_fusion
  328.6 2.5 slice_bitcast_fusion
  (3 shorter events, 0.0 us)
Async XLA Ops:
  7.2 1.3 copy-start
  7.2 2.6 copy-start.6
  7.2 2.6 copy-start.8
  7.2 296.6 %all-reduce.2.cloned.1.call-start = ((), (), s32[]{:S(2)}) async-start(), calls=%async_computation | async-start | bytes 6291456 | tf_op jit(solution)/shard_map/psum | solution.py:58
  8.4 1.7 copy-start.7
  8.4 1.7 copy-start.10
  14.2 0.9 copy-start.9
  303.8 2.8 copy-start.1
  309.9 2.6 copy-start.2
  314.6 2.6 copy-start.3
  319.2 2.6 copy-start.4
  323.8 2.6 copy-start.5
Sparse Core Ops, SparseCore 0:
  14.4 289.3 all-reduce.1
where the time goes:
time: 338 us
  waiting for transfers between devices  287 us (85%)
  matrix products  25.9 us (8%)
  between operations  14.3 us (4%)
  local copies, waits for them, and re-layouts  6.1 us (2%)
  other arithmetic  4.93 us (1%)
    psum x1, waiting for transfers between devices, per_device(): total = lax.psum(stacked, 'seq')  287 us
    dot_general x5, matrix products, newton_batch(): jnp.einsum('mdf,mef->mde', xmat, xmat, preferred_element_type=jnp.float32)  11 us
    dot_general x5, matrix products, newton_batch(): jnp.einsum('mde,mef->mdf', bmat, xmat, preferred_element_type=jnp.float32)  10.2 us
  transfers between devices with their start and end apart: 1, of which 1 were waited for; matrix products, arithmetic and copies ran while one was open for 1% of the time, Pallas kernels for 0%

commit v1 on v0

v1 whole, which is shorter than its diff:
```python
import math

import jax
import jax.numpy as jnp
from jax import lax
from jax.experimental import pallas as pl
from jax.experimental.pallas import tpu as pltpu
from jax.sharding import PartitionSpec as P

NS_STEPS = 5
NX = 4
NZ = 16
GROUPS = 3
PER = 2
F32 = jnp.float32
BF16 = jnp.bfloat16
MESH = pl.DeviceIdType.MESH


def dot(a, b, ca, cb):
    return lax.dot_general(a, b, (((ca,), (cb,)), ((), ())), preferred_element_type=F32)


def sigmoid(x):
    return 0.5 * jnp.tanh(0.5 * x) + 0.5


def slot_of(head, kind):
    if kind == 2:
        return 0, head
    return 1 + head, kind


def grads_kernel(q_ref, k_ref, v_ref, r_ref, wg_ref, wu_ref, wd_ref, app_ref, g_ref):
    heads, dh, hid = wg_ref.shape
    s1, s2 = dh ** (-0.5), hid ** (-0.5)
    rates = jnp.transpose(r_ref[...])
    half = hid // 2
    for h in range(heads):
        cols = slice(h * dh, (h + 1) * dh)
        q, k = q_ref[:, cols], k_ref[:, cols]
        vr = (rates[:, h : h + 1] * v_ref[:, cols].astype(F32)).astype(BF16)
        kt = jnp.transpose(k)
        vt = jnp.transpose(vr)
        acc = None
        for j in range(2):
            js = slice(j * half, (j + 1) * half)
            wg, wu, wd = wg_ref[h, :, js], wu_ref[h, :, js], wd_ref[h, js, :]
            gk = s1 * dot(k, wg, 1, 0)
            uk = s1 * dot(k, wu, 1, 0)
            dhid = -s2 * dot(vr, wd, 1, 1)
            sig = sigmoid(gk)
            silu = gk * sig
            hk = (silu * uk).astype(BF16)
            dg = (dhid * uk * (sig * (1.0 + gk * (1.0 - sig)))).astype(BF16)
            du = (dhid * silu).astype(BF16)
            for kind, lhs, rhs, scale in ((2, vt, hk, -s2), (0, kt, dg, s1), (1, kt, du, s1)):
                out = (scale * dot(lhs, rhs, 1, 0)).astype(BF16)
                group, place = slot_of(h, kind)
                for c in range(2):
                    g_ref[group, 2 * j + c, place] = out[:, c * 128 : (c + 1) * 128]
            gq = s1 * dot(q, wg, 1, 0)
            uq = s1 * dot(q, wu, 1, 0)
            hq = (gq * sigmoid(gq) * uq).astype(BF16)
            part = dot(hq, wd, 1, 0)
            acc = part if acc is None else acc + part
        app_ref[:, cols] = (s2 * acc).astype(BF16)


def wait_all(ref, sem):
    pltpu.make_async_copy(ref, ref, sem).wait()


def reduce_kernel(g_ref, o_ref, xr, zs, zr, sems):
    me = lax.axis_index("seq")
    z, x = me // NX, me % NX

    def along_x(d):
        return z * NX + (x + d) % NX

    def along_z(d):
        return ((z + d) % NZ) * NX + x

    def send(src, dst, kind, group, peer):
        pltpu.make_async_remote_copy(
            src_ref=src,
            dst_ref=dst,
            send_sem=sems.at[kind, group],
            recv_sem=sems.at[4 + kind, group],
            device_id={"seq": peer},
            device_id_type=MESH,
        ).start()

    barrier = pltpu.get_barrier_semaphore()
    for d in range(1, NX):
        pl.semaphore_signal(barrier, inc=1, device_id={"seq": along_x(d)}, device_id_type=MESH)
    for d in range(1, NZ):
        pl.semaphore_signal(barrier, inc=1, device_id={"seq": along_z(d)}, device_id_type=MESH)
    pl.semaphore_wait(barrier, NX + NZ - 2)

    mine = pl.ds(pl.multiple_of(z * 16, 16), 16)
    for g in range(GROUPS):
        for d in (2, 1, 3):
            send(g_ref.at[g, (x + d) % NX], xr.at[g, d - 1], 0, g, along_x(d))
    for g in range(GROUPS):
        wait_all(xr.at[g], sems.at[4, g])
        total = g_ref[g, x].astype(F32)
        for d in range(NX - 1):
            total = total + xr[g, d].astype(F32)
        zs[g] = total.astype(BF16)
        for d in (8, 7, 9, 6, 10, 5, 11, 4, 12, 3, 13, 2, 14, 1, 15):
            theirs = pl.ds(pl.multiple_of(((z + d) % NZ) * 16, 16), 16)
            send(zs.at[g, :, theirs], zr.at[g, d - 1], 1, g, along_z(d))
    for g in range(GROUPS):
        wait_all(zr.at[g], sems.at[5, g])
        total = zs[g, :, mine].astype(F32)
        for d in range(NZ - 1):
            total = total + zr[g, d].astype(F32)
        o_ref[g, x, :, mine] = total.astype(BF16)
        for d in (8, 7, 9, 6, 10, 5, 11, 4, 12, 3, 13, 2, 14, 1, 15):
            chunk = o_ref.at[g, x, :, mine]
            send(chunk, chunk, 2, g, along_z(d))
    for g in range(GROUPS):
        wait_all(zr.at[g], sems.at[6, g])
        for d in (2, 1, 3):
            send(o_ref.at[g, x], o_ref.at[g, x], 3, g, along_x(d))
    for g in range(GROUPS):
        wait_all(xr.at[g], sems.at[7, g])
    for g in range(GROUPS):
        wait_all(xr.at[g], sems.at[0, g])
        wait_all(zr.at[g], sems.at[1, g])
        wait_all(zr.at[g], sems.at[2, g])
        wait_all(xr.at[g], sems.at[3, g])


def newton_kernel(t_ref, gate_ref, up_ref, down_ref, x_ref):
    outs = (gate_ref, up_ref, down_ref)
    heads, _, hid = gate_ref.shape
    where = [(h, kind) for h in range(heads) for kind in (2, 0, 1)]
    for m, (h, kind) in enumerate(where):
        group, place = slot_of(h, kind)
        total = jnp.concatenate(
            [t_ref[group, c, place].astype(F32) for c in range(NX)], axis=1
        )
        norm = jnp.sqrt(jnp.sum(total * total, keepdims=True)) + 1e-07
        x_ref[m] = (total / norm).astype(BF16)

    def step(s, carry):
        scale = jnp.where(s == NS_STEPS - 1, 0.2 * math.sqrt(hid), 1.0).astype(F32)
        for m in range(len(where)):
            x = x_ref[m]
            a = dot(x, x, 1, 1).astype(BF16)
            b = (-4.775 * a.astype(F32) + 2.0315 * dot(a, a, 1, 0)).astype(BF16)
            nxt = 3.4445 * x.astype(F32) + dot(b, x, 1, 0)
            x_ref[m] = (nxt * scale).astype(BF16)
        return carry

    lax.fori_loop(0, NS_STEPS, step, 0)
    for m, (h, kind) in enumerate(where):
        outs[kind][h] = x_ref[m]


def per_device(queries, keys, values, token_rates, w_gate, w_up, w_down):
    heads, dh, hid = w_gate.shape
    tokens = queries.shape[0]
    vmem = pl.BlockSpec(memory_space=pltpu.VMEM)
    travel = jax.ShapeDtypeStruct((GROUPS, NX, PER, dh, hid // NX), BF16)
    applied, grads = pl.pallas_call(
        grads_kernel,
        name="grads",
        out_shape=(jax.ShapeDtypeStruct((tokens, heads * dh), BF16), travel),
        in_specs=[vmem] * 7,
        out_specs=(vmem, vmem),
        compiler_params=pltpu.CompilerParams(vmem_limit_bytes=24 << 20),
    )(queries, keys, values, token_rates, w_gate, w_up, w_down)
    total = pl.pallas_call(
        reduce_kernel,
        name="reduce",
        out_shape=travel,
        in_specs=[vmem],
        out_specs=vmem,
        scratch_shapes=[
            pltpu.VMEM((GROUPS, NX - 1, PER, dh, hid // NX), BF16),
            pltpu.VMEM((GROUPS, PER, dh, hid // NX), BF16),
            pltpu.VMEM((GROUPS, NZ - 1, PER, dh // NZ, hid // NX), BF16),
            pltpu.SemaphoreType.DMA((8, GROUPS)),
        ],
        compiler_params=pltpu.CompilerParams(
            collective_id=0, has_side_effects=True, vmem_limit_bytes=24 << 20
        ),
    )(grads)
    weights = jax.ShapeDtypeStruct((heads, dh, hid), BF16)
    gate, up, down = pl.pallas_call(
        newton_kernel,
        name="newton",
        out_shape=(weights,) * 3,
        in_specs=[vmem],
        out_specs=(vmem,) * 3,
        scratch_shapes=[pltpu.VMEM((heads * 3, dh, hid), BF16)],
        compiler_params=pltpu.CompilerParams(vmem_limit_bytes=24 << 20),
    )(total)
    return (applied, gate, up, down)


def solution(mesh):
    in_specs = (
        P("seq", "head"),
        P("seq", "head"),
        P("seq", "head"),
        P("head", "seq"),
        P("head", None, None),
        P("head", None, None),
        P("head", None, None),
    )
    out_specs = (
        P("seq", "head"),
        P("head", None, None),
        P("head", None, None),
        P("head", None, None),
    )
    return jax.shard_map(
        per_device, mesh=mesh, in_specs=in_specs, out_specs=out_specs, check_vma=False
    )
```

time: 338 us -> 94.3 us (0.28)
  waiting for transfers between devices: 287 us -> 0 us
  Pallas kernels: 0 us -> 86.4 us
  matrix products: 25.9 us -> 0 us
  between operations: 14.3 us -> 0.66 us
  other arithmetic: 4.93 us -> 0 us
    psum x1 -> x0, waiting for transfers between devices: 287 us -> none  [per_device(): total = lax.psum(stacked, 'seq')]
    pallas_call x0 -> x3, Pallas kernels: none -> 86.4 us  [the longest x1 67.5 us: per_device(): pl.pallas_call(reduce_kernel, name='reduce', out_shape=travel, in_specs=[...]
    dot_general x18 -> x0, matrix products: 25.9 us -> none  [the longest x5 11 us: newton_batch(): jnp.einsum('mdf,mef->mde', xmat, xmat, preferred_element_type=jnp.float32)]
    unnamed x23 -> x14, local copies, waits for them, and re-layouts: 2.23 us -> 6.65 us
  transfers between devices with their start and end apart: 1 -> 0, of which waited for: 1 -> 0; matrix products, arithmetic and copies ran while one was open for 1% -> 0% of each run, Pallas kernels for 0% -> 0%
where the time goes in v1:
time: 94.3 us; the launch traced here: 93.7 us
  Pallas kernels  86.4 us (92%)
  local copies, waits for them, and re-layouts  6.65 us (7%)
    pallas_call x1, Pallas kernels, per_device(): pl.pallas_call(reduce_kernel, name='reduce', out_shape=travel, in_specs=[...  67.5 us
    pallas_call x1, Pallas kernels, per_device(): pl.pallas_call(newton_kernel, name='newton', out_shape=(weights,) * 3, in...  15.8 us
    unnamed x14, local copies, waits for them, and re-layouts  6.65 us
    pallas_call x1, Pallas kernels, per_device(): pl.pallas_call(grads_kernel, name='grads', out_shape=(jax.ShapeDtypeStruc...  3.16 us

profile of v1, /device:TPU:24, one launch (start us, length us, event | category | flops | bytes accessed | tf_op | source)
XLA Modules:
  0.0 93.7 jit_solution(2690712834756610377)
XLA Ops:
  0.6 0.0 copy-start
  0.6 1.0 %copy-done = bf16[2,256,512]{2,1,0:T(8,128)(2,1)S(1)} copy-done((bf16[2,256,512]{2,1,0:T(8,128)(2,1)S(1)}, bf16[2,256,512]{2,1,0:T(8,128)(2,1)}, u32[]{:S(2)}) %copy-start) | copy-done | bytes 524312
  1.7 0.0 copy-start.1
  1.7 1.0 %copy-done.1 = bf16[2,256,512]{2,1,0:T(8,128)(2,1)S(1)} copy-done((bf16[2,256,512]{2,1,0:T(8,128)(2,1)S(1)}, bf16[2,256,512]{2,1,0:T(8,128)(2,1)}, u32[]{:S(2)}) %copy-start.1) | copy-done | bytes 524312
  2.7 0.0 copy-start.2
  2.7 1.0 %copy-done.2 = bf16[2,512,256]{2,1,0:T(8,128)(2,1)S(1)} copy-done((bf16[2,512,256]{2,1,0:T(8,128)(2,1)S(1)}, bf16[2,512,256]{2,1,0:T(8,128)(2,1)}, u32[]{:S(2)}) %copy-start.2) | copy-done | bytes 524312
  3.8 0.0 copy-start.3
  3.8 0.9 %copy-done.3 = bf16[256,512]{1,0:T(8,128)(2,1)S(1)} copy-done((bf16[256,512]{1,0:T(8,128)(2,1)S(1)}, bf16[256,512]{1,0:T(8,128)(2,1)}, u32[]{:S(2)}) %copy-start.3) | copy-done | bytes 262168
  4.7 0.0 copy-start.4
  4.7 0.9 %copy-done.4 = bf16[256,512]{1,0:T(8,128)(2,1)S(1)} copy-done((bf16[256,512]{1,0:T(8,128)(2,1)S(1)}, bf16[256,512]{1,0:T(8,128)(2,1)}, u32[]{:S(2)}) %copy-start.4) | copy-done | bytes 262168
  5.7 0.0 copy-start.5
  5.7 0.9 %copy-done.5 = bf16[256,512]{1,0:T(8,128)(2,1)S(1)} copy-done((bf16[256,512]{1,0:T(8,128)(2,1)S(1)}, bf16[256,512]{1,0:T(8,128)(2,1)}, u32[]{:S(2)}) %copy-start.5) | copy-done | bytes 262168
  6.6 0.0 copy-start.6
  6.6 0.7 copy-done.6
  7.3 3.2 %grads.1 = (bf16[256,512]{1,0:T(8,128)(2,1)}, bf16[3,4,2,256,128]{4,3,2,1,0:T(8,128)(2,1)S(1)}) custom-call(bf16[256,512]{1,0:T(8,128)(2,1)S(1)} %copy-done.3, bf16[256,512]{1,0:T(8,128)(2,1)S(1)} %copy-done.4, bf16[256,512]{1,0:T(8,128)(2,1)S(1)} %copy-done.5, f32[2,256]{1,0:T(2,128)S(1)} %copy-done.6, bf16[2,256,512]{2,1,0:T(8,128)(2,1)S(1)} %copy-done, ...), custom_call_target="tpu_custom_call" | custom-call | tf_op jit(solution)/shard_map/grads/pallas_call | solution.py:168
  10.4 67.5 %reduce.1.t_ref = bf16[3,4,2,256,128]{4,3,2,1,0:T(8,128)(2,1)S(1)} custom-call(bf16[3,4,2,256,128]{4,3,2,1,0:T(8,128)(2,1)S(1)} %get-tuple-element.10.g_ref), custom_call_target="tpu_custom_call" | custom-call | tf_op jit(solution)/shard_map/reduce/pallas_call | solution.py:176
  77.9 15.8 %newton.1 = (bf16[2,256,512]{2,1,0:T(8,128)(2,1)}, bf16[2,256,512]{2,1,0:T(8,128)(2,1)}, bf16[2,256,512]{2,1,0:T(8,128)(2,1)}) custom-call(bf16[3,4,2,256,128]{4,3,2,1,0:T(8,128)(2,1)S(1)} %reduce.1.t_ref), custom_call_target="tpu_custom_call" | custom-call | tf_op jit(solution)/shard_map/newton/pallas_call | solution.py:193
Async XLA Ops:
  0.6 1.0 %copy-start = (bf16[2,256,512]{2,1,0:T(8,128)(2,1)S(1)}, bf16[2,256,512]{2,1,0:T(8,128)(2,1)}, u32[]{:S(2)}) copy-start(bf16[2,256,512]{2,1,0:T(8,128)(2,1)} %wg_ref.1) | copy-start | bytes 1572868
  1.7 1.0 %copy-start.1 = (bf16[2,256,512]{2,1,0:T(8,128)(2,1)S(1)}, bf16[2,256,512]{2,1,0:T(8,128)(2,1)}, u32[]{:S(2)}) copy-start(bf16[2,256,512]{2,1,0:T(8,128)(2,1)} %wu_ref.1) | copy-start | bytes 1572868
  2.7 1.0 %copy-start.2 = (bf16[2,512,256]{2,1,0:T(8,128)(2,1)S(1)}, bf16[2,512,256]{2,1,0:T(8,128)(2,1)}, u32[]{:S(2)}) copy-start(bf16[2,512,256]{2,1,0:T(8,128)(2,1)} %wd_ref.1) | copy-start | bytes 1572868
  3.8 0.9 %copy-start.3 = (bf16[256,512]{1,0:T(8,128)(2,1)S(1)}, bf16[256,512]{1,0:T(8,128)(2,1)}, u32[]{:S(2)}) copy-start(bf16[256,512]{1,0:T(8,128)(2,1)} %q_ref.1) | copy-start | bytes 786436
  4.7 0.9 %copy-start.4 = (bf16[256,512]{1,0:T(8,128)(2,1)S(1)}, bf16[256,512]{1,0:T(8,128)(2,1)}, u32[]{:S(2)}) copy-start(bf16[256,512]{1,0:T(8,128)(2,1)} %k_ref.1) | copy-start | bytes 786436
  5.7 0.9 %copy-start.5 = (bf16[256,512]{1,0:T(8,128)(2,1)S(1)}, bf16[256,512]{1,0:T(8,128)(2,1)}, u32[]{:S(2)}) copy-start(bf16[256,512]{1,0:T(8,128)(2,1)} %v_ref.1) | copy-start | bytes 786436
  6.6 0.7 copy-start.6

commit v2 on v0

v2 whole, which is shorter than its diff:
```python
import math

import jax
import jax.numpy as jnp
from jax import lax
from jax.experimental import pallas as pl
from jax.experimental.pallas import tpu as pltpu
from jax.sharding import PartitionSpec as P

NS_STEPS = 5
NX = 4
NZ = 16
GROUPS = 3
PER = 2
F32 = jnp.float32
BF16 = jnp.bfloat16
MESH = pl.DeviceIdType.MESH


def dot(a, b, ca, cb):
    return lax.dot_general(a, b, (((ca,), (cb,)), ((), ())), preferred_element_type=F32)


def sigmoid(x):
    return 0.5 * jnp.tanh(0.5 * x) + 0.5


def wait_all(ref, sem):
    pltpu.make_async_copy(ref, ref, sem).wait()


def token_grads(k, vr, wg, wu, wd, s1, s2):
    gk = s1 * dot(k, wg, 1, 0)
    uk = s1 * dot(k, wu, 1, 0)
    dhid = -s2 * dot(vr, wd, 1, 1)
    sig = sigmoid(gk)
    silu = gk * sig
    hk = (silu * uk).astype(BF16)
    dg = (dhid * uk * (sig * (1.0 + gk * (1.0 - sig)))).astype(BF16)
    du = (dhid * silu).astype(BF16)
    kt = jnp.transpose(k)
    return (
        -s2 * dot(jnp.transpose(vr), hk, 1, 0),
        s1 * dot(kt, dg, 1, 0),
        s1 * dot(kt, du, 1, 0),
    )


def head_apply(h, q, wg, wu, wd):
    dh, hid = wg.shape[1:]
    s1, s2 = dh ** (-0.5), hid ** (-0.5)
    half = hid // 2
    total = None
    for j in range(2):
        js = slice(j * half, (j + 1) * half)
        gq = s1 * dot(q, wg[h, :, js], 1, 0)
        uq = s1 * dot(q, wu[h, :, js], 1, 0)
        hq = (gq * sigmoid(gq) * uq).astype(BF16)
        part = dot(hq, wd[h, js, :], 1, 0)
        total = part if total is None else total + part
    return (s2 * total).astype(BF16)


TOKENS, NEAR, FAR, SPREAD, FILL, SIDE, PASS = range(7)
KINDS = 7
STRIDE = 5
STEPS = (1, 2, -1, -2)
LATENCY, INTERVAL = 3.0, 1.0


def main_kernel(
    q_hbm, k_hbm, v_hbm, r_hbm, wg_hbm, wu_hbm, wd_hbm, app_ref, o_ref,
    q_ref, k_ref, v_ref, r_ref, wg, wu, wd, wg_own, wu_own, wd_own, kv, acc, own,
    near, got, far, spread, loads, sems,
):
    heads, dh, hid = wg.shape
    s1, s2 = dh ** (-0.5), hid ** (-0.5)
    me = lax.axis_index("seq")
    z, x = me // NX, me % NX
    right, left_x = (x + 1) % NX, (x + NX - 1) % NX
    split = NX // heads
    own_head = x // split
    part = pl.ds(pl.multiple_of((x % split) * (hid // split), hid // split), hid // split)

    def along_x(d):
        return z * NX + (x + d) % NX

    def along_z(d):
        return ((z + d) % NZ) * NX + x

    def send(src, dst, kind, group, peer):
        pltpu.make_async_remote_copy(
            src_ref=src,
            dst_ref=dst,
            send_sem=sems.at[kind, group],
            recv_sem=sems.at[KINDS + kind, group],
            device_id={"seq": peer},
            device_id_type=MESH,
        ).start()

    def arrived(ref, kind, group):
        wait_all(ref, sems.at[KINDS + kind, group])

    def left(ref, kind, group):
        wait_all(ref, sems.at[kind, group])

    def rows(d):
        return pl.ds(pl.multiple_of(((z + d) % NZ) * 16, 16), 16)

    copies = [(r_hbm, r_ref), (v_hbm, v_ref)]
    copies += [(k_hbm.at[:, pl.ds(h * dh, dh)], k_ref.at[0, h]) for h in range(heads)]
    copies += [
        (wg_hbm.at[own_head, :, part], wg_own),
        (wu_hbm.at[own_head, :, part], wu_own),
        (wd_hbm.at[own_head, part], wd_own),
        (q_hbm, q_ref),
        (wg_hbm, wg),
        (wu_hbm, wu),
        (wd_hbm, wd),
    ]
    copies = [pltpu.make_async_copy(a, b, loads.at[i]) for i, (a, b) in enumerate(copies)]
    for copy in copies:
        copy.start()
    barrier = pltpu.get_barrier_semaphore()
    peers = [along_x(d) for d in (1, 2, 3)]
    peers += [along_z(d) for d in (1, -1, 2, -2, 3, -3, 5, -5)]
    for peer in peers:
        pl.semaphore_signal(barrier, inc=1, device_id={"seq": peer}, device_id_type=MESH)

    def start_z(g):
        def chunk(d):
            return own[g, :, rows(d)]

        for j, t in enumerate(STEPS):
            for i in range(3):
                near[g, 3 * j + i] = chunk(t + STRIDE * (i - 1))
            send(near.at[g, pl.ds(3 * j, 3)], got.at[g, pl.ds(3 * j, 3)], NEAR, g, along_z(t))
        near[g, 12] = chunk(-8)
        send(near.at[g, 12], got.at[g, 12], NEAR, g, along_z(-3))
        for i in range(3):
            near[g, 13 + i] = chunk(STRIDE * (i - 1))

    def collect(g):
        arrived(got.at[g], NEAR, g)
        for i in (0, 2, 1):
            total = near[g, 13 + i].astype(F32)
            for j in range(4):
                total = total + got[g, 3 * j + i].astype(F32)
            if i == 0:
                total = total + got[g, 12].astype(F32)
            near[g, 13 + i] = total.astype(BF16)
            if i != 1:
                send(near.at[g, 13 + i], far.at[g, i // 2], FAR, g, along_z(STRIDE * (i - 1)))

    def finish_sum(g):
        arrived(far.at[g], FAR, g)
        total = near[g, 14].astype(F32) + far[g, 0].astype(F32) + far[g, 1].astype(F32)
        spread[g, 1] = total.astype(BF16)
        send(spread.at[g, 1], spread.at[g, 2], SPREAD, g, along_z(-STRIDE))
        send(spread.at[g, 1], spread.at[g, 0], SPREAD, g, along_z(STRIDE))

    def fill(g):
        arrived(far.at[g], SPREAD, g)
        for j, t in enumerate(STEPS):
            mine = spread.at[g, pl.ds(0, 3)]
            send(mine, spread.at[g, pl.ds(3 + 3 * j, 3)], FILL, g, along_z(t))
        send(spread.at[g, 0], spread.at[g, 15], FILL, g, along_z(3))

    def side(g):
        arrived(got.at[g], FILL, g)
        for j, t in enumerate((0,) + STEPS):
            for i in range(3):
                o_ref[g, x, :, rows(STRIDE * (i - 1) - t)] = spread[g, 3 * j + i]
        o_ref[g, x, :, rows(8)] = spread[g, 15]
        for d in (1, -1):
            send(o_ref.at[g, x], o_ref.at[g, x], SIDE, g, along_x(d))

    def pass_on(g):
        arrived(o_ref.at[g, pl.ds(0, 2)], SIDE, g)
        send(o_ref.at[g, left_x, 0], o_ref.at[g, left_x, 0], PASS, g, along_x(1))
        send(o_ref.at[g, right, 1], o_ref.at[g, right, 1], PASS, g, along_x(-1))

    def end(g):
        arrived(o_ref.at[g, 0], PASS, g)

    for copy in copies[: 2 + heads]:
        copy.wait()
    rates = jnp.transpose(r_ref[...])
    for h in range(heads):
        v = v_ref[:, h * dh : (h + 1) * dh].astype(F32)
        k_ref[1, h] = (rates[:, h : h + 1] * v).astype(BF16)
    pl.semaphore_wait(barrier, len(peers))
    for i in range(2):
        for d in (2, 1, 3):
            theirs = k_ref.at[i, (x + d) % NX // split]
            send(theirs, kv.at[d - 1, i], TOKENS, d - 1, along_x(d))
    for copy in copies[2 + heads : 5 + heads]:
        copy.wait()
    weights = (wg_own[...], wu_own[...], wd_own[...], s1, s2)
    for g, grad in enumerate(token_grads(k_ref[0, own_head], k_ref[1, own_head], *weights)):
        acc[g] = grad
    for copy in copies[5 + heads :]:
        copy.wait()
    for h in range(heads):
        cols = slice(h * dh, (h + 1) * dh)
        app_ref[:, cols] = head_apply(h, q_ref[:, cols], wg, wu, wd)
    for d in (1, 3):
        arrived(kv.at[d - 1], TOKENS, d - 1)
        for g, grad in enumerate(token_grads(kv[d - 1, 0], kv[d - 1, 1], *weights)):
            acc[g] = acc[g] + grad
    arrived(kv.at[1], TOKENS, 1)
    for g, grad in enumerate(token_grads(kv[1, 0], kv[1, 1], *weights)):
        total = (acc[g] + grad).astype(BF16)
        for c in range(PER):
            own[g, c] = total[:, c * 128 : (c + 1) * 128]
        start_z(g)
    stages = (collect, finish_sum, fill, side, pass_on, end)
    order = sorted(
        (LATENCY * s + INTERVAL * g, s, g) for s in range(len(stages)) for g in range(GROUPS)
    )
    for _, s, g in order:
        stages[s](g)
    for g in range(GROUPS):
        left(kv.at[g], TOKENS, g)
        left(got.at[g], NEAR, g)
        left(far.at[g], FAR, g)
        left(far.at[g], SPREAD, g)
        left(got.at[g], FILL, g)
        left(o_ref.at[g, pl.ds(0, 2)], SIDE, g)
        left(o_ref.at[g, 0], PASS, g)


def newton_kernel(
    t_ref, applied_ref, applied_hbm, gate_hbm, up_hbm, down_hbm, x_ref, a_ref, sems
):
    outs = (gate_hbm, up_hbm, down_hbm)
    heads, _, hid = gate_hbm.shape
    handed = pltpu.make_async_copy(applied_ref, applied_hbm, sems.at[heads * 3])
    handed.start()
    where = [(h, kind) for h in range(heads) for kind in (2, 0, 1)]
    for m, (h, kind) in enumerate(where):
        blocks = [divmod(i, PER) for i in range(hid // 128)]
        split = NX // heads
        total = jnp.concatenate(
            [t_ref[(kind + 1) % 3, split * h + c, i].astype(F32) for c, i in blocks], axis=1
        )
        norm = jnp.sqrt(jnp.sum(total * total, keepdims=True)) + 1e-07
        x_ref[m] = (total / norm).astype(BF16)

    for s in range(NS_STEPS):
        for m in range(len(where)):
            x = x_ref[m]
            a_ref[m] = dot(x, x, 1, 1).astype(BF16)
        for m in range(len(where)):
            a = a_ref[m]
            b = -4.775 * a.astype(F32) + 2.0315 * dot(a, a, 1, 0)
            a_ref[m] = b.astype(BF16)
        for m in range(len(where)):
            x = x_ref[m]
            nxt = 3.4445 * x.astype(F32) + dot(a_ref[m], x, 1, 0)
            if s == NS_STEPS - 1:
                nxt = nxt * (0.2 * math.sqrt(hid))
            x_ref[m] = nxt.astype(BF16)
            if s == NS_STEPS - 1:
                h, kind = where[m]
                pltpu.make_async_copy(x_ref.at[m], outs[kind].at[h], sems.at[m]).start()
    for m, (h, kind) in enumerate(where):
        pltpu.make_async_copy(x_ref.at[m], outs[kind].at[h], sems.at[m]).wait()
    handed.wait()


def per_device(queries, keys, values, token_rates, w_gate, w_up, w_down):
    heads, dh, hid = w_gate.shape
    tokens = queries.shape[0]
    vmem = pl.BlockSpec(memory_space=pltpu.VMEM)
    hbm = pl.BlockSpec(memory_space=pltpu.HBM)
    tile = (dh // NZ, hid // NX)
    half = hid * heads // NX
    travel = jax.ShapeDtypeStruct((GROUPS, NX, PER, dh, hid // NX), BF16)
    out = jax.ShapeDtypeStruct((tokens, heads * dh), BF16)
    weights = jax.ShapeDtypeStruct((heads, dh, hid), BF16)
    given = (queries, keys, values, token_rates, w_gate, w_up, w_down)
    given = [pltpu.with_memory_space_constraint(a, pltpu.HBM) for a in given]
    applied, total = pl.pallas_call(
        main_kernel,
        name="grads_and_sum",
        out_shape=(out, travel),
        in_specs=[hbm] * 7,
        out_specs=(vmem, vmem),
        scratch_shapes=[
            pltpu.VMEM(queries.shape, BF16),
            pltpu.VMEM((2, heads, tokens, dh), BF16),
            pltpu.VMEM(values.shape, BF16),
            pltpu.VMEM(token_rates.shape, F32),
            pltpu.VMEM(w_gate.shape, BF16),
            pltpu.VMEM(w_up.shape, BF16),
            pltpu.VMEM(w_down.shape, BF16),
            pltpu.VMEM((dh, half), BF16),
            pltpu.VMEM((dh, half), BF16),
            pltpu.VMEM((half, dh), BF16),
            pltpu.VMEM((NX - 1, 2, tokens, dh), BF16),
            pltpu.VMEM((GROUPS, dh, half), F32),
            pltpu.VMEM((GROUPS, PER, dh, hid // NX), BF16),
            pltpu.VMEM((GROUPS, 16, PER) + tile, BF16),
            pltpu.VMEM((GROUPS, 13, PER) + tile, BF16),
            pltpu.VMEM((GROUPS, 2, PER) + tile, BF16),
            pltpu.VMEM((GROUPS, 16, PER) + tile, BF16),
            pltpu.SemaphoreType.DMA((9 + heads,)),
            pltpu.SemaphoreType.DMA((2 * KINDS, GROUPS)),
        ],
        compiler_params=pltpu.CompilerParams(
            collective_id=0, has_side_effects=True, vmem_limit_bytes=32 << 20
        ),
    )(*given)
    return pl.pallas_call(
        newton_kernel,
        name="newton",
        out_shape=(out, weights, weights, weights),
        in_specs=[vmem, vmem],
        out_specs=(hbm,) * 4,
        scratch_shapes=[
            pltpu.VMEM((heads * 3, dh, hid), BF16),
            pltpu.VMEM((heads * 3, dh, dh), BF16),
            pltpu.SemaphoreType.DMA((heads * 3 + 1,)),
        ],
        compiler_params=pltpu.CompilerParams(vmem_limit_bytes=24 << 20),
    )(total, applied)


def solution(mesh):
    in_specs = (
        P("seq", "head"),
        P("seq", "head"),
        P("seq", "head"),
        P("head", "seq"),
        P("head", None, None),
        P("head", None, None),
        P("head", None, None),
    )
    out_specs = (
        P("seq", "head"),
        P("head", None, None),
        P("head", None, None),
        P("head", None, None),
    )
    return jax.shard_map(
        per_device, mesh=mesh, in_specs=in_specs, out_specs=out_specs, check_vma=False
    )
```

time: 338 us -> 74.2 us (0.22)
  waiting for transfers between devices: 287 us -> 0 us
  Pallas kernels: 0 us -> 73.3 us
  matrix products: 25.9 us -> 0 us
  between operations: 14.3 us -> 0.64 us
  local copies, waits for them, and re-layouts: 6.1 us -> 0 us
  other arithmetic: 4.93 us -> 0 us
    psum x1 -> x0, waiting for transfers between devices: 287 us -> none  [per_device(): total = lax.psum(stacked, 'seq')]
    pallas_call x0 -> x2, Pallas kernels: none -> 73.3 us  [the longest x1 66.1 us: per_device(): pl.pallas_call(main_kernel, name='grads_and_sum', out_shape=(out, travel)...]
    dot_general x18 -> x0, matrix products: 25.9 us -> none  [the longest x5 11 us: newton_batch(): jnp.einsum('mdf,mef->mde', xmat, xmat, preferred_element_type=jnp.float32)]
  transfers between devices with their start and end apart: 1 -> 0, of which waited for: 1 -> 0; matrix products, arithmetic and copies ran while one was open for 1% -> 0% of each run, Pallas kernels for 0% -> 0%
where the time goes in v2:
time: 74.2 us; the launch traced here: 74 us
  Pallas kernels  73.3 us (99%)
    pallas_call x1, Pallas kernels, per_device(): pl.pallas_call(main_kernel, name='grads_and_sum', out_shape=(out, travel)...  66.1 us
    pallas_call x1, Pallas kernels, per_device(): pl.pallas_call(newton_kernel, name='newton', out_shape=(out, weights, wei...  7.23 us

profile of v2, /device:TPU:24, one launch (start us, length us, event | category | flops | bytes accessed | tf_op | source)
XLA Modules:
  0.0 74.0 jit_solution(5056601352566578782)
XLA Ops:
  0.6 66.1 %grads_and_sum.1 = (bf16[256,512]{1,0:T(8,128)(2,1)S(1)}, bf16[3,4,2,256,128]{4,3,2,1,0:T(8,128)(2,1)S(1)}) custom-call(bf16[256,512]{1,0:T(8,128)(2,1)} %q_hbm.1, bf16[256,512]{1,0:T(8,128)(2,1)} %k_hbm.1, bf16[256,512]{1,0:T(8,128)(2,1)} %v_hbm.1, f32[2,256]{1,0:T(2,128)} %r_hbm.1, bf16[2,256,512]{2,1,0:T(8,128)(2,1)} %wg_hbm.1, ...), custom_call_target="tpu_custom_call" | custom-call | tf_op jit(solution)/shard_map/grads_and_sum/pallas_call | solution.py:284
  66.7 7.2 %newton.1 = (bf16[256,512]{1,0:T(8,128)(2,1)}, bf16[2,256,512]{2,1,0:T(8,128)(2,1)}, bf16[2,256,512]{2,1,0:T(8,128)(2,1)}, bf16[2,256,512]{2,1,0:T(8,128)(2,1)}) custom-call(bf16[3,4,2,256,128]{4,3,2,1,0:T(8,128)(2,1)S(1)} %get-tuple-element.6.t_ref, bf16[256,512]{1,0:T(8,128)(2,1)S(1)} %get-tuple-element.7.applied_ref), custom_call_target="tpu_custom_call" | custom-call | tf_op jit(solution)/shard_map/newton/pallas_call | solution.py:315

commit v3 on v2

--- a/solution.py
+++ b/solution.py
@@ -61,7 +61,7 @@
     return (s2 * total).astype(BF16)
 
 
-TOKENS, NEAR, FAR, SPREAD, FILL, SIDE, PASS = range(7)
+TOKENS, RELAY, NEAR, FAR, FILL, SIDE, PASS = range(7)
 KINDS = 7
 STRIDE = 5
 STEPS = (1, 2, -1, -2)
@@ -71,7 +71,7 @@
 def main_kernel(
     q_hbm, k_hbm, v_hbm, r_hbm, wg_hbm, wu_hbm, wd_hbm, app_ref, o_ref,
     q_ref, k_ref, v_ref, r_ref, wg, wu, wd, wg_own, wu_own, wd_own, kv, acc, own,
-    near, got, far, spread, loads, sems,
+    relay, near, got, far, spread, loads, sems,
 ):
     heads, dh, hid = wg.shape
     s1, s2 = dh ** (-0.5), hid ** (-0.5)
@@ -79,8 +79,8 @@
     z, x = me // NX, me % NX
     right, left_x = (x + 1) % NX, (x + NX - 1) % NX
     split = NX // heads
-    own_head = x // split
-    part = pl.ds(pl.multiple_of((x % split) * (hid // split), hid // split), hid // split)
+    own_head, other_head = x % heads, (x + 1) % heads
+    part = pl.ds(pl.multiple_of((x // heads) * (hid // split), hid // split), hid // split)
 
     def along_x(d):
         return z * NX + (x + d) % NX
@@ -107,8 +107,8 @@
     def rows(d):
         return pl.ds(pl.multiple_of(((z + d) % NZ) * 16, 16), 16)
 
-    copies = [(r_hbm, r_ref), (v_hbm, v_ref)]
-    copies += [(k_hbm.at[:, pl.ds(h * dh, dh)], k_ref.at[0, h]) for h in range(heads)]
+    copies = [(k_hbm.at[:, pl.ds(h * dh, dh)], k_ref.at[0, h]) for h in range(heads)]
+    copies += [(r_hbm, r_ref), (v_hbm, v_ref)]
     copies += [
         (wg_hbm.at[own_head, :, part], wg_own),
         (wu_hbm.at[own_head, :, part], wu_own),
@@ -122,8 +122,8 @@
     for copy in copies:
         copy.start()
     barrier = pltpu.get_barrier_semaphore()
-    peers = [along_x(d) for d in (1, 2, 3)]
-    peers += [along_z(d) for d in (1, -1, 2, -2, 3, -3, 5, -5)]
+    peers = [along_x(d) for d in (1, -1)]
+    peers += [along_z(d) for d in (1, -1, 2, -2, 3, -3, 5, -5, 6, -6)]
     for peer in peers:
         pl.semaphore_signal(barrier, inc=1, device_id={"seq": peer}, device_id_type=MESH)
 
@@ -149,18 +149,17 @@
             if i == 0:
                 total = total + got[g, 12].astype(F32)
             near[g, 13 + i] = total.astype(BF16)
-            if i != 1:
-                send(near.at[g, 13 + i], far.at[g, i // 2], FAR, g, along_z(STRIDE * (i - 1)))
-
-    def finish_sum(g):
+        send(near.at[g, pl.ds(14, 2)], far.at[g, pl.ds(0, 2)], FAR, g, along_z(STRIDE))
+        send(near.at[g, pl.ds(13, 2)], far.at[g, pl.ds(2, 2)], FAR, g, along_z(-STRIDE))
+        send(near.at[g, 13], far.at[g, 4], FAR, g, along_z(-2 * STRIDE))
+        send(near.at[g, 15], far.at[g, 5], FAR, g, along_z(2 * STRIDE))
+
+    def fill(g):
         arrived(far.at[g], FAR, g)
-        total = near[g, 14].astype(F32) + far[g, 0].astype(F32) + far[g, 1].astype(F32)
-        spread[g, 1] = total.astype(BF16)
-        send(spread.at[g, 1], spread.at[g, 2], SPREAD, g, along_z(-STRIDE))
-        send(spread.at[g, 1], spread.at[g, 0], SPREAD, g, along_z(STRIDE))
-
-    def fill(g):
-        arrived(far.at[g], SPREAD, g)
+        parts = ((far[g, 5], far[g, 0], near[g, 13]), (far[g, 1], near[g, 14], far[g, 2]))
+        parts += ((near[g, 15], far[g, 3], far[g, 4]),)
+        for i, (a, b, c) in enumerate(parts):
+            spread[g, i] = (a.astype(F32) + b.astype(F32) + c.astype(F32)).astype(BF16)
         for j, t in enumerate(STEPS):
             mine = spread.at[g, pl.ds(0, 3)]
             send(mine, spread.at[g, pl.ds(3 + 3 * j, 3)], FILL, g, along_z(t))
@@ -183,22 +182,30 @@
     def end(g):
         arrived(o_ref.at[g, 0], PASS, g)
 
-    for copy in copies[: 2 + heads]:
+    def send_tokens(i, relayed):
+        send(k_ref.at[i, own_head], relay.at[i], RELAY, i, along_x(relayed))
+        for d in (1, 3):
+            send(k_ref.at[i, other_head], kv.at[d - 1, i], TOKENS, d - 1, along_x(d))
+
+    for copy in copies[:heads]:
+        copy.wait()
+    pl.semaphore_wait(barrier, len(peers))
+    send_tokens(0, 1)
+    for copy in copies[heads : heads + 2]:
         copy.wait()
     rates = jnp.transpose(r_ref[...])
     for h in range(heads):
         v = v_ref[:, h * dh : (h + 1) * dh].astype(F32)
         k_ref[1, h] = (rates[:, h : h + 1] * v).astype(BF16)
-    pl.semaphore_wait(barrier, len(peers))
-    for i in range(2):
-        for d in (2, 1, 3):
-            theirs = k_ref.at[i, (x + d) % NX // split]
-            send(theirs, kv.at[d - 1, i], TOKENS, d - 1, along_x(d))
+    send_tokens(1, -1)
     for copy in copies[2 + heads : 5 + heads]:
         copy.wait()
     weights = (wg_own[...], wu_own[...], wd_own[...], s1, s2)
     for g, grad in enumerate(token_grads(k_ref[0, own_head], k_ref[1, own_head], *weights)):
         acc[g] = grad
+    for i, d in ((0, 1), (1, -1)):
+        arrived(relay.at[i], RELAY, i)
+        send(relay.at[i], kv.at[1, i], TOKENS, 1, along_x(d))
     for copy in copies[5 + heads :]:
         copy.wait()
     for h in range(heads):
@@ -214,17 +221,18 @@
         for c in range(PER):
             own[g, c] = total[:, c * 128 : (c + 1) * 128]
         start_z(g)
-    stages = (collect, finish_sum, fill, side, pass_on, end)
+    stages = (collect, fill, side, pass_on, end)
     order = sorted(
         (LATENCY * s + INTERVAL * g, s, g) for s in range(len(stages)) for g in range(GROUPS)
     )
     for _, s, g in order:
         stages[s](g)
+    for i in range(2):
+        left(relay.at[i], RELAY, i)
     for g in range(GROUPS):
         left(kv.at[g], TOKENS, g)
         left(got.at[g], NEAR, g)
         left(far.at[g], FAR, g)
-        left(far.at[g], SPREAD, g)
         left(got.at[g], FILL, g)
         left(o_ref.at[g, pl.ds(0, 2)], SIDE, g)
         left(o_ref.at[g, 0], PASS, g)
@@ -240,9 +248,8 @@
     where = [(h, kind) for h in range(heads) for kind in (2, 0, 1)]
     for m, (h, kind) in enumerate(where):
         blocks = [divmod(i, PER) for i in range(hid // 128)]
-        split = NX // heads
         total = jnp.concatenate(
-            [t_ref[(kind + 1) % 3, split * h + c, i].astype(F32) for c, i in blocks], axis=1
+            [t_ref[(kind + 1) % 3, heads * c + h, i].astype(F32) for c, i in blocks], axis=1
         )
         norm = jnp.sqrt(jnp.sum(total * total, keepdims=True)) + 1e-07
         x_ref[m] = (total / norm).astype(BF16)
@@ -301,9 +308,10 @@
             pltpu.VMEM((NX - 1, 2, tokens, dh), BF16),
             pltpu.VMEM((GROUPS, dh, half), F32),
             pltpu.VMEM((GROUPS, PER, dh, hid // NX), BF16),
+            pltpu.VMEM((2, tokens, dh), BF16),
             pltpu.VMEM((GROUPS, 16, PER) + tile, BF16),
             pltpu.VMEM((GROUPS, 13, PER) + tile, BF16),
-            pltpu.VMEM((GROUPS, 2, PER) + tile, BF16),
+            pltpu.VMEM((GROUPS, 6, PER) + tile, BF16),
             pltpu.VMEM((GROUPS, 16, PER) + tile, BF16),
             pltpu.SemaphoreType.DMA((9 + heads,)),
             pltpu.SemaphoreType.DMA((2 * KINDS, GROUPS)),

time: 74.2 us -> 70 us (0.943)
  Pallas kernels: 73.3 us -> 69.3 us
    pallas_call x1, Pallas kernels: 66.1 us -> 62 us  [per_device(): pl.pallas_call(main_kernel, name='grads_and_sum', out_shape=(out, travel)...]
where the time goes in v3:
time: 70 us; the launch traced here: 69.9 us
  Pallas kernels  69.3 us (99%)
    pallas_call x1, Pallas kernels, per_device(): pl.pallas_call(main_kernel, name='grads_and_sum', out_shape=(out, travel)...  62 us
    pallas_call x1, Pallas kernels, per_device(): pl.pallas_call(newton_kernel, name='newton', out_shape=(out, weights, wei...  7.23 us

profile of v3, /device:TPU:24, one launch (start us, length us, event | category | flops | bytes accessed | tf_op | source)
XLA Modules:
  0.0 69.9 jit_solution(15707779142825448775)
XLA Ops:
  0.6 62.0 %grads_and_sum.1 = (bf16[256,512]{1,0:T(8,128)(2,1)S(1)}, bf16[3,4,2,256,128]{4,3,2,1,0:T(8,128)(2,1)S(1)}) custom-call(bf16[256,512]{1,0:T(8,128)(2,1)} %q_hbm.1, bf16[256,512]{1,0:T(8,128)(2,1)} %k_hbm.1, bf16[256,512]{1,0:T(8,128)(2,1)} %v_hbm.1, f32[2,256]{1,0:T(2,128)} %r_hbm.1, bf16[2,256,512]{2,1,0:T(8,128)(2,1)} %wg_hbm.1, ...), custom_call_target="tpu_custom_call" | custom-call | tf_op jit(solution)/shard_map/grads_and_sum/pallas_call | solution.py:291
  62.7 7.2 %newton.1 = (bf16[256,512]{1,0:T(8,128)(2,1)}, bf16[2,256,512]{2,1,0:T(8,128)(2,1)}, bf16[2,256,512]{2,1,0:T(8,128)(2,1)}, bf16[2,256,512]{2,1,0:T(8,128)(2,1)}) custom-call(bf16[3,4,2,256,128]{4,3,2,1,0:T(8,128)(2,1)S(1)} %get-tuple-element.6.t_ref, bf16[256,512]{1,0:T(8,128)(2,1)S(1)} %get-tuple-element.7.applied_ref), custom_call_target="tpu_custom_call" | custom-call | tf_op jit(solution)/shard_map/newton/pallas_call | solution.py:323

commit v4 on v3

--- a/solution.py
+++ b/solution.py
@@ -10,8 +10,9 @@
 NS_STEPS = 5
 NX = 4
 NZ = 16
-GROUPS = 3
-PER = 2
+GROUPS = 6
+PER = 1
+SLOTS = 6
 F32 = jnp.float32
 BF16 = jnp.bfloat16
 MESH = pl.DeviceIdType.MESH
@@ -61,17 +62,16 @@
     return (s2 * total).astype(BF16)
 
 
-TOKENS, RELAY, NEAR, FAR, FILL, SIDE, PASS = range(7)
-KINDS = 7
+TOKENS, RATES, RELAY, NEAR, FAR, FILL, SIDE, PASS = range(8)
+KINDS = 8
 STRIDE = 5
 STEPS = (1, 2, -1, -2)
-LATENCY, INTERVAL = 3.0, 1.0
 
 
 def main_kernel(
     q_hbm, k_hbm, v_hbm, r_hbm, wg_hbm, wu_hbm, wd_hbm, app_ref, o_ref,
-    q_ref, k_ref, v_ref, r_ref, wg, wu, wd, wg_own, wu_own, wd_own, kv, acc, own,
-    relay, near, got, far, spread, loads, sems,
+    q_ref, wg, wu, wd, wg_own, wu_own, wd_own, kv, rates, acc, own,
+    relay, near, got, far, spread, loads, sems, beyond,
 ):
     heads, dh, hid = wg.shape
     s1, s2 = dh ** (-0.5), hid ** (-0.5)
@@ -107,25 +107,28 @@
     def rows(d):
         return pl.ds(pl.multiple_of(((z + d) % NZ) * 16, 16), 16)
 
-    copies = [(k_hbm.at[:, pl.ds(h * dh, dh)], k_ref.at[0, h]) for h in range(heads)]
-    copies += [(r_hbm, r_ref), (v_hbm, v_ref)]
-    copies += [
+    own_cols = pl.ds(pl.multiple_of(own_head * dh, dh), dh)
+    other_cols = pl.ds(pl.multiple_of(other_head * dh, dh), dh)
+    copies = [
+        (k_hbm.at[:, own_cols], kv.at[0, 0]),
         (wg_hbm.at[own_head, :, part], wg_own),
         (wu_hbm.at[own_head, :, part], wu_own),
+        (v_hbm.at[:, own_cols], kv.at[0, 1]),
+        (r_hbm, rates.at[0]),
         (wd_hbm.at[own_head, part], wd_own),
         (q_hbm, q_ref),
         (wg_hbm, wg),
         (wu_hbm, wu),
         (wd_hbm, wd),
     ]
+    barrier = pltpu.get_barrier_semaphore()
+    peers = [along_x(d) for d in (1, -1)]
+    peers += [along_z(d) for d in (1, -1, 2, -2, 3, -3)]
+    for peer in peers:
+        pl.semaphore_signal(barrier, inc=1, device_id={"seq": peer}, device_id_type=MESH)
     copies = [pltpu.make_async_copy(a, b, loads.at[i]) for i, (a, b) in enumerate(copies)]
     for copy in copies:
         copy.start()
-    barrier = pltpu.get_barrier_semaphore()
-    peers = [along_x(d) for d in (1, -1)]
-    peers += [along_z(d) for d in (1, -1, 2, -2, 3, -3, 5, -5, 6, -6)]
-    for peer in peers:
-        pl.semaphore_signal(barrier, inc=1, device_id={"seq": peer}, device_id_type=MESH)
 
     def start_z(g):
         def chunk(d):
@@ -176,61 +179,71 @@
 
     def pass_on(g):
         arrived(o_ref.at[g, pl.ds(0, 2)], SIDE, g)
-        send(o_ref.at[g, left_x, 0], o_ref.at[g, left_x, 0], PASS, g, along_x(1))
-        send(o_ref.at[g, right, 1], o_ref.at[g, right, 1], PASS, g, along_x(-1))
+        for origin, at, d in ((left_x, 0, 1), (right, dh // 2, -1)):
+            piece = o_ref.at[g, origin, :, pl.ds(at, dh // 2)]
+            send(piece, piece, PASS, g, along_x(d))
 
     def end(g):
         arrived(o_ref.at[g, 0], PASS, g)
 
-    def send_tokens(i, relayed):
-        send(k_ref.at[i, own_head], relay.at[i], RELAY, i, along_x(relayed))
+    pl.semaphore_wait(barrier, len(peers))
+    for d in (3, -3):
+        pl.semaphore_signal(
+            beyond, inc=1, device_id={"seq": along_z(d)}, device_id_type=MESH
+        )
+    for i, (array, d) in enumerate(((k_hbm, 1), (v_hbm, -1))):
+        send(array.at[:, own_cols], relay.at[i], RELAY, i, along_x(d))
+    send(r_hbm, rates.at[1], RATES, 1, along_x(1))
+    send(r_hbm, rates.at[3], RATES, 3, along_x(-1))
+    for i, array in enumerate((k_hbm, v_hbm)):
         for d in (1, 3):
-            send(k_ref.at[i, other_head], kv.at[d - 1, i], TOKENS, d - 1, along_x(d))
-
-    for copy in copies[:heads]:
-        copy.wait()
-    pl.semaphore_wait(barrier, len(peers))
-    send_tokens(0, 1)
-    for copy in copies[heads : heads + 2]:
-        copy.wait()
-    rates = jnp.transpose(r_ref[...])
-    for h in range(heads):
-        v = v_ref[:, h * dh : (h + 1) * dh].astype(F32)
-        k_ref[1, h] = (rates[:, h : h + 1] * v).astype(BF16)
-    send_tokens(1, -1)
-    for copy in copies[2 + heads : 5 + heads]:
+            send(array.at[:, other_cols], kv.at[d, i], TOKENS, d, along_x(d))
+    for copy in copies[:6]:
         copy.wait()
     weights = (wg_own[...], wu_own[...], wd_own[...], s1, s2)
-    for g, grad in enumerate(token_grads(k_ref[0, own_head], k_ref[1, own_head], *weights)):
-        acc[g] = grad
-    for i, d in ((0, 1), (1, -1)):
-        arrived(relay.at[i], RELAY, i)
-        send(relay.at[i], kv.at[1, i], TOKENS, 1, along_x(d))
-    for copy in copies[5 + heads :]:
+
+    def grads_from(d):
+        rate = jnp.transpose(rates[d])
+        rate = jnp.where(own_head == 0, rate[:, 0:1], rate[:, 1:2])
+        vr = (rate * kv[d, 1].astype(F32)).astype(BF16)
+        return enumerate(token_grads(kv[d, 0], vr, *weights))
+
+    for i, grad in grads_from(0):
+        acc[i] = grad
+    for copy in copies[6:]:
         copy.wait()
     for h in range(heads):
         cols = slice(h * dh, (h + 1) * dh)
         app_ref[:, cols] = head_apply(h, q_ref[:, cols], wg, wu, wd)
+    arrived(rates.at[1], RATES, 1)
+    send(rates.at[1], rates.at[2], RATES, 2, along_x(1))
+    for i, d in ((0, 1), (1, -1)):
+        arrived(relay.at[i], RELAY, i)
+        send(relay.at[i], kv.at[2, i], TOKENS, 2, along_x(d))
+    arrived(rates.at[3], RATES, 3)
     for d in (1, 3):
-        arrived(kv.at[d - 1], TOKENS, d - 1)
-        for g, grad in enumerate(token_grads(kv[d - 1, 0], kv[d - 1, 1], *weights)):
-            acc[g] = acc[g] + grad
-    arrived(kv.at[1], TOKENS, 1)
-    for g, grad in enumerate(token_grads(kv[1, 0], kv[1, 1], *weights)):
-        total = (acc[g] + grad).astype(BF16)
-        for c in range(PER):
-            own[g, c] = total[:, c * 128 : (c + 1) * 128]
-        start_z(g)
+        arrived(kv.at[d], TOKENS, d)
+        for i, grad in grads_from(d):
+            acc[i] = acc[i] + grad
+    arrived(rates.at[2], RATES, 2)
+    arrived(kv.at[2], TOKENS, 2)
+    for i, grad in grads_from(2):
+        total = (acc[i] + grad).astype(BF16)
+        for c in range(2):
+            own[divmod(2 * i + c, PER)] = total[:, c * 128 : (c + 1) * 128]
+            if (2 * i + c + 1) % PER == 0:
+                start_z((2 * i + c) // PER)
+    pl.semaphore_wait(beyond, 2)
     stages = (collect, fill, side, pass_on, end)
-    order = sorted(
-        (LATENCY * s + INTERVAL * g, s, g) for s in range(len(stages)) for g in range(GROUPS)
-    )
-    for _, s, g in order:
-        stages[s](g)
+    for stage in stages:
+        for g in range(GROUPS):
+            stage(g)
     for i in range(2):
         left(relay.at[i], RELAY, i)
+    for d in range(1, NX):
+        left(kv.at[d], TOKENS, d)
+        left(rates.at[d], RATES, d)
     for g in range(GROUPS):
-        left(kv.at[g], TOKENS, g)
         left(got.at[g], NEAR, g)
         left(far.at[g], FAR, g)
         left(got.at[g], FILL, g)
@@ -246,18 +259,22 @@
     handed = pltpu.make_async_copy(applied_ref, applied_hbm, sems.at[heads * 3])
     handed.start()
     where = [(h, kind) for h in range(heads) for kind in (2, 0, 1)]
+    norms = []
     for m, (h, kind) in enumerate(where):
-        blocks = [divmod(i, PER) for i in range(hid // 128)]
-        total = jnp.concatenate(
-            [t_ref[(kind + 1) % 3, heads * c + h, i].astype(F32) for c, i in blocks], axis=1
-        )
-        norm = jnp.sqrt(jnp.sum(total * total, keepdims=True)) + 1e-07
-        x_ref[m] = (total / norm).astype(BF16)
-
+        blocks = []
+        for c in range(hid // 128):
+            group, place = divmod(2 * ((kind + 1) % 3) + c % 2, PER)
+            blocks.append(t_ref[group, heads * (c // 2) + h, place].astype(F32))
+        total = jnp.concatenate(blocks, axis=1)
+        norms.append(jnp.sqrt(jnp.sum(total * total, keepdims=True)) + 1e-07)
+        x_ref[m] = total.astype(BF16)
     for s in range(NS_STEPS):
         for m in range(len(where)):
             x = x_ref[m]
-            a_ref[m] = dot(x, x, 1, 1).astype(BF16)
+            square = dot(x, x, 1, 1)
+            if s == 0:
+                square = square * (1.0 / norms[m]) * (1.0 / norms[m])
+            a_ref[m] = square.astype(BF16)
         for m in range(len(where)):
             a = a_ref[m]
             b = -4.775 * a.astype(F32) + 2.0315 * dot(a, a, 1, 0)
@@ -265,6 +282,8 @@
         for m in range(len(where)):
             x = x_ref[m]
             nxt = 3.4445 * x.astype(F32) + dot(a_ref[m], x, 1, 0)
+            if s == 0:
+                nxt = nxt * (1.0 / norms[m])
             if s == NS_STEPS - 1:
                 nxt = nxt * (0.2 * math.sqrt(hid))
             x_ref[m] = nxt.astype(BF16)
@@ -296,25 +315,24 @@
         out_specs=(vmem, vmem),
         scratch_shapes=[
             pltpu.VMEM(queries.shape, BF16),
-            pltpu.VMEM((2, heads, tokens, dh), BF16),
-            pltpu.VMEM(values.shape, BF16),
-            pltpu.VMEM(token_rates.shape, F32),
             pltpu.VMEM(w_gate.shape, BF16),
             pltpu.VMEM(w_up.shape, BF16),
             pltpu.VMEM(w_down.shape, BF16),
             pltpu.VMEM((dh, half), BF16),
             pltpu.VMEM((dh, half), BF16),
             pltpu.VMEM((half, dh), BF16),
-            pltpu.VMEM((NX - 1, 2, tokens, dh), BF16),
-            pltpu.VMEM((GROUPS, dh, half), F32),
+            pltpu.VMEM((NX, 2, tokens, dh), BF16),
+            pltpu.VMEM((NX,) + token_rates.shape, F32),
+            pltpu.VMEM((3, dh, half), F32),
             pltpu.VMEM((GROUPS, PER, dh, hid // NX), BF16),
             pltpu.VMEM((2, tokens, dh), BF16),
             pltpu.VMEM((GROUPS, 16, PER) + tile, BF16),
             pltpu.VMEM((GROUPS, 13, PER) + tile, BF16),
             pltpu.VMEM((GROUPS, 6, PER) + tile, BF16),
             pltpu.VMEM((GROUPS, 16, PER) + tile, BF16),
-            pltpu.SemaphoreType.DMA((9 + heads,)),
-            pltpu.SemaphoreType.DMA((2 * KINDS, GROUPS)),
+            pltpu.SemaphoreType.DMA((10,)),
+            pltpu.SemaphoreType.DMA((2 * KINDS, SLOTS)),
+            pltpu.SemaphoreType.REGULAR,
         ],
         compiler_params=pltpu.CompilerParams(
             collective_id=0, has_side_effects=True, vmem_limit_bytes=32 << 20

time: 70 us -> 67 us (0.957)
  Pallas kernels: 69.3 us -> 66.2 us
    pallas_call x1, Pallas kernels: 62 us -> 59.3 us  [per_device(): pl.pallas_call(main_kernel, name='grads_and_sum', out_shape=(out, travel)...]
where the time goes in v4:
time: 67 us; the launch traced here: 66.9 us
  Pallas kernels  66.2 us (99%)
    pallas_call x1, Pallas kernels, per_device(): pl.pallas_call(main_kernel, name='grads_and_sum', out_shape=(out, travel)...  59.3 us
    pallas_call x1, Pallas kernels, per_device(): pl.pallas_call(newton_kernel, name='newton', out_shape=(out, weights, wei...  6.95 us

profile of v4, /device:TPU:24, one launch (start us, length us, event | category | flops | bytes accessed | tf_op | source)
XLA Modules:
  0.0 66.9 jit_solution(13673294393998594267)
XLA Ops:
  0.6 59.3 %grads_and_sum.1 = (bf16[256,512]{1,0:T(8,128)(2,1)S(1)}, bf16[6,4,1,256,128]{4,3,2,1,0:T(8,128)(2,1)S(1)}) custom-call(bf16[256,512]{1,0:T(8,128)(2,1)} %q_hbm.1, bf16[256,512]{1,0:T(8,128)(2,1)} %k_hbm.1, bf16[256,512]{1,0:T(8,128)(2,1)} %v_hbm.1, f32[2,256]{1,0:T(2,128)} %r_hbm.1, bf16[2,256,512]{2,1,0:T(8,128)(2,1)} %wg_hbm.1, ...), custom_call_target="tpu_custom_call" | custom-call | tf_op jit(solution)/shard_map/grads_and_sum/pallas_call | solution.py:310
  59.9 6.9 %newton.1 = (bf16[256,512]{1,0:T(8,128)(2,1)}, bf16[2,256,512]{2,1,0:T(8,128)(2,1)}, bf16[2,256,512]{2,1,0:T(8,128)(2,1)}, bf16[2,256,512]{2,1,0:T(8,128)(2,1)}) custom-call(bf16[6,4,1,256,128]{4,3,2,1,0:T(8,128)(2,1)S(1)} %get-tuple-element.6.t_ref, bf16[256,512]{1,0:T(8,128)(2,1)S(1)} %get-tuple-element.7.applied_ref), custom_call_target="tpu_custom_call" | custom-call | tf_op jit(solution)/shard_map/newton/pallas_call | solution.py:341

commit v5 on v4

--- a/solution.py
+++ b/solution.py
@@ -8,6 +8,8 @@
 from jax.sharding import PartitionSpec as P
 
 NS_STEPS = 5
+HEAD_START = 2
+ORDER = (2, 0, 1)
 NX = 4
 NZ = 16
 GROUPS = 6
@@ -69,9 +71,9 @@
 
 
 def main_kernel(
-    q_hbm, k_hbm, v_hbm, r_hbm, wg_hbm, wu_hbm, wd_hbm, app_ref, o_ref,
+    q_hbm, k_hbm, v_hbm, r_hbm, wg_hbm, wu_hbm, wd_hbm, app_ref, o_ref, begun_ref,
     q_ref, wg, wu, wd, wg_own, wu_own, wd_own, kv, rates, acc, own,
-    relay, near, got, far, spread, loads, sems, beyond,
+    relay, near, got, far, spread, a_ref, loads, sems, beyond,
 ):
     heads, dh, hid = wg.shape
     s1, s2 = dh ** (-0.5), hid ** (-0.5)
@@ -234,10 +236,21 @@
             if (2 * i + c + 1) % PER == 0:
                 start_z((2 * i + c) // PER)
     pl.semaphore_wait(beyond, 2)
-    stages = (collect, fill, side, pass_on, end)
+    stages = (collect, fill, side, pass_on)
     for stage in stages:
         for g in range(GROUPS):
             stage(g)
+    early = begun_ref.shape[0]
+    ready = GROUPS * early // (3 * heads)
+    for g in range(ready):
+        end(g)
+    where = [(h, kind) for kind in ORDER for h in range(heads)]
+    scales = [newton_start(o_ref, begun_ref, m, *where[m], heads) for m in range(early)]
+    for s in range(HEAD_START):
+        for _ in newton_step(begun_ref, a_ref, range(early), s, scales):
+            pass
+    for g in range(ready, GROUPS):
+        end(g)
     for i in range(2):
         left(relay.at[i], RELAY, i)
     for d in range(1, NX):
@@ -251,42 +264,56 @@
         left(o_ref.at[g, 0], PASS, g)
 
 
+def newton_start(t_ref, x_ref, m, h, kind, heads):
+    blocks = []
+    for c in range(NX):
+        group, place = divmod(2 * ((kind + 1) % 3) + c % 2, PER)
+        blocks.append(t_ref[group, heads * (c // 2) + h, place].astype(F32))
+    total = jnp.concatenate(blocks, axis=1)
+    x_ref[m] = total.astype(BF16)
+    return 1.0 / (jnp.sqrt(jnp.sum(total * total, keepdims=True)) + 1e-07)
+
+
+def newton_step(x_ref, a_ref, mats, s, scales):
+    for m in mats:
+        x = x_ref[m]
+        square = dot(x, x, 1, 1)
+        if s == 0:
+            square = square * scales[m] * scales[m]
+        a_ref[m] = square.astype(BF16)
+    for m in mats:
+        a = a_ref[m]
+        a_ref[m] = (-4.775 * a.astype(F32) + 2.0315 * dot(a, a, 1, 0)).astype(BF16)
+    for m in mats:
+        x = x_ref[m]
+        nxt = 3.4445 * x.astype(F32) + dot(a_ref[m], x, 1, 0)
+        if s == 0:
+            nxt = nxt * scales[m]
+        if s == NS_STEPS - 1:
+            nxt = nxt * (0.2 * math.sqrt(x.shape[1]))
+        x_ref[m] = nxt.astype(BF16)
+        yield m
+
+
 def newton_kernel(
-    t_ref, applied_ref, applied_hbm, gate_hbm, up_hbm, down_hbm, x_ref, a_ref, sems
+    t_ref, begun_ref, applied_ref, applied_hbm, gate_hbm, up_hbm, down_hbm, x_ref, a_ref, sems
 ):
     outs = (gate_hbm, up_hbm, down_hbm)
-    heads, _, hid = gate_hbm.shape
+    heads = gate_hbm.shape[0]
     handed = pltpu.make_async_copy(applied_ref, applied_hbm, sems.at[heads * 3])
     handed.start()
-    where = [(h, kind) for h in range(heads) for kind in (2, 0, 1)]
-    norms = []
-    for m, (h, kind) in enumerate(where):
-        blocks = []
-        for c in range(hid // 128):
-            group, place = divmod(2 * ((kind + 1) % 3) + c % 2, PER)
-            blocks.append(t_ref[group, heads * (c // 2) + h, place].astype(F32))
-        total = jnp.concatenate(blocks, axis=1)
-        norms.append(jnp.sqrt(jnp.sum(total * total, keepdims=True)) + 1e-07)
-        x_ref[m] = total.astype(BF16)
+    where = [(h, kind) for kind in ORDER for h in range(heads)]
+    early = begun_ref.shape[0]
+    scales = {}
+    for m in range(early, len(where)):
+        scales[m] = newton_start(t_ref, x_ref, m, *where[m], heads)
     for s in range(NS_STEPS):
-        for m in range(len(where)):
-            x = x_ref[m]
-            square = dot(x, x, 1, 1)
-            if s == 0:
-                square = square * (1.0 / norms[m]) * (1.0 / norms[m])
-            a_ref[m] = square.astype(BF16)
-        for m in range(len(where)):
-            a = a_ref[m]
-            b = -4.775 * a.astype(F32) + 2.0315 * dot(a, a, 1, 0)
-            a_ref[m] = b.astype(BF16)
-        for m in range(len(where)):
-            x = x_ref[m]
-            nxt = 3.4445 * x.astype(F32) + dot(a_ref[m], x, 1, 0)
-            if s == 0:
-                nxt = nxt * (1.0 / norms[m])
-            if s == NS_STEPS - 1:
-                nxt = nxt * (0.2 * math.sqrt(hid))
-            x_ref[m] = nxt.astype(BF16)
+        mats = range(early, len(where))
+        if s >= HEAD_START:
+            mats = range(len(where))
+        if s == HEAD_START:
+            x_ref[pl.ds(0, early)] = begun_ref[...]
+        for m in newton_step(x_ref, a_ref, mats, s, scales):
             if s == NS_STEPS - 1:
                 h, kind = where[m]
                 pltpu.make_async_copy(x_ref.at[m], outs[kind].at[h], sems.at[m]).start()
@@ -307,12 +334,13 @@
     weights = jax.ShapeDtypeStruct((heads, dh, hid), BF16)
     given = (queries, keys, values, token_rates, w_gate, w_up, w_down)
     given = [pltpu.with_memory_space_constraint(a, pltpu.HBM) for a in given]
-    applied, total = pl.pallas_call(
+    begun = jax.ShapeDtypeStruct((heads * 2, dh, hid), BF16)
+    applied, total, begun = pl.pallas_call(
         main_kernel,
         name="grads_and_sum",
-        out_shape=(out, travel),
+        out_shape=(out, travel, begun),
         in_specs=[hbm] * 7,
-        out_specs=(vmem, vmem),
+        out_specs=(vmem,) * 3,
         scratch_shapes=[
             pltpu.VMEM(queries.shape, BF16),
             pltpu.VMEM(w_gate.shape, BF16),
@@ -330,6 +358,7 @@
             pltpu.VMEM((GROUPS, 13, PER) + tile, BF16),
             pltpu.VMEM((GROUPS, 6, PER) + tile, BF16),
             pltpu.VMEM((GROUPS, 16, PER) + tile, BF16),
+            pltpu.VMEM((heads * 2, dh, dh), BF16),
             pltpu.SemaphoreType.DMA((10,)),
             pltpu.SemaphoreType.DMA((2 * KINDS, SLOTS)),
             pltpu.SemaphoreType.REGULAR,
@@ -342,7 +371,7 @@
         newton_kernel,
         name="newton",
         out_shape=(out, weights, weights, weights),
-        in_specs=[vmem, vmem],
+        in_specs=[vmem] * 3,
         out_specs=(hbm,) * 4,
         scratch_shapes=[
             pltpu.VMEM((heads * 3, dh, hid), BF16),
@@ -350,7 +379,7 @@
             pltpu.SemaphoreType.DMA((heads * 3 + 1,)),
         ],
         compiler_params=pltpu.CompilerParams(vmem_limit_bytes=24 << 20),
-    )(total, applied)
+    )(total, begun, applied)
 
 
 def solution(mesh):

time: 67 us -> 66.2 us (0.988)
  Pallas kernels: 66.2 us -> 65.4 us
    pallas_call x1, Pallas kernels: 6.95 us -> 5.67 us  [per_device(): pl.pallas_call(newton_kernel, name='newton', out_shape=(out, weights, wei...]
where the time goes in v5:
time: 66.2 us; the launch traced here: 66.1 us
  Pallas kernels  65.4 us (99%)
    pallas_call x1, Pallas kernels, per_device(): pl.pallas_call(main_kernel, name='grads_and_sum', out_shape=(out, travel,...  59.7 us
    pallas_call x1, Pallas kernels, per_device(): pl.pallas_call(newton_kernel, name='newton', out_shape=(out, weights, wei...  5.67 us

profile of v5, /device:TPU:24, one launch (start us, length us, event | category | flops | bytes accessed | tf_op | source)
XLA Modules:
  0.0 66.1 jit_solution(16197931148651615105)
XLA Ops:
  0.6 59.7 %grads_and_sum.1 = (bf16[256,512]{1,0:T(8,128)(2,1)S(1)}, bf16[6,4,1,256,128]{4,3,2,1,0:T(8,128)(2,1)S(1)}, bf16[4,256,512]{2,1,0:T(8,128)(2,1)S(1)}) custom-call(bf16[256,512]{1,0:T(8,128)(2,1)} %q_hbm.1, bf16[256,512]{1,0:T(8,128)(2,1)} %k_hbm.1, bf16[256,512]{1,0:T(8,128)(2,1)} %v_hbm.1, f32[2,256]{1,0:T(2,128)} %r_hbm.1, bf16[2,256,512]{2,1,0:T(8,128)(2,1)} %wg_hbm.1, ...), custom_call_target="tpu_custom_call" | custom-call | tf_op jit(solution)/shard_map/grads_and_sum/pallas_call | solution.py:338
  60.4 5.7 %newton.1 = (bf16[256,512]{1,0:T(8,128)(2,1)}, bf16[2,256,512]{2,1,0:T(8,128)(2,1)}, bf16[2,256,512]{2,1,0:T(8,128)(2,1)}, bf16[2,256,512]{2,1,0:T(8,128)(2,1)}) custom-call(bf16[6,4,1,256,128]{4,3,2,1,0:T(8,128)(2,1)S(1)} %get-tuple-element.7.t_ref, bf16[4,256,512]{2,1,0:T(8,128)(2,1)S(1)} %get-tuple-element.8.begun_ref, ...), custom_call_target="tpu_custom_call" | custom-call | tf_op jit(solution)/shard_map/newton/pallas_call | solution.py:370

commit v6 on v5

--- a/solution.py
+++ b/solution.py
@@ -125,7 +125,7 @@
     ]
     barrier = pltpu.get_barrier_semaphore()
     peers = [along_x(d) for d in (1, -1)]
-    peers += [along_z(d) for d in (1, -1, 2, -2, 3, -3)]
+    peers += [along_z(d) for d in (1, -1, 2, -2)]
     for peer in peers:
         pl.semaphore_signal(barrier, inc=1, device_id={"seq": peer}, device_id_type=MESH)
     copies = [pltpu.make_async_copy(a, b, loads.at[i]) for i, (a, b) in enumerate(copies)]
@@ -189,10 +189,13 @@
         arrived(o_ref.at[g, 0], PASS, g)
 
     pl.semaphore_wait(barrier, len(peers))
-    for d in (3, -3):
-        pl.semaphore_signal(
-            beyond, inc=1, device_id={"seq": along_z(d)}, device_id_type=MESH
-        )
+    def tell(at, distance):
+        for d in (distance, -distance):
+            pl.semaphore_signal(
+                beyond.at[at], inc=1, device_id={"seq": along_z(d)}, device_id_type=MESH
+            )
+
+    tell(0, 2)
     for i, (array, d) in enumerate(((k_hbm, 1), (v_hbm, -1))):
         send(array.at[:, own_cols], relay.at[i], RELAY, i, along_x(d))
     send(r_hbm, rates.at[1], RATES, 1, along_x(1))
@@ -227,6 +230,8 @@
         arrived(kv.at[d], TOKENS, d)
         for i, grad in grads_from(d):
             acc[i] = acc[i] + grad
+    pl.semaphore_wait(beyond.at[0], 2)
+    tell(1, 3)
     arrived(rates.at[2], RATES, 2)
     arrived(kv.at[2], TOKENS, 2)
     for i, grad in grads_from(2):
@@ -235,7 +240,7 @@
             own[divmod(2 * i + c, PER)] = total[:, c * 128 : (c + 1) * 128]
             if (2 * i + c + 1) % PER == 0:
                 start_z((2 * i + c) // PER)
-    pl.semaphore_wait(beyond, 2)
+    pl.semaphore_wait(beyond.at[1], 2)
     stages = (collect, fill, side, pass_on)
     for stage in stages:
         for g in range(GROUPS):
@@ -361,7 +366,7 @@
             pltpu.VMEM((heads * 2, dh, dh), BF16),
             pltpu.SemaphoreType.DMA((10,)),
             pltpu.SemaphoreType.DMA((2 * KINDS, SLOTS)),
-            pltpu.SemaphoreType.REGULAR,
+            pltpu.SemaphoreType.REGULAR((2,)),
         ],
         compiler_params=pltpu.CompilerParams(
             collective_id=0, has_side_effects=True, vmem_limit_bytes=32 << 20

time: 66.2 us -> 66.3 us (level)
  no operation moved by 1% of the time
where the time goes in v6:
time: 66.3 us; the launch traced here: 66.2 us
  Pallas kernels  65.5 us (99%)
    pallas_call x1, Pallas kernels, per_device(): pl.pallas_call(main_kernel, name='grads_and_sum', out_shape=(out, travel,...  59.9 us
    pallas_call x1, Pallas kernels, per_device(): pl.pallas_call(newton_kernel, name='newton', out_shape=(out, weights, wei...  5.68 us

profile of v6, /device:TPU:24, one launch (start us, length us, event | category | flops | bytes accessed | tf_op | source)
XLA Modules:
  0.0 66.2 jit_solution(10765413830232883076)
XLA Ops:
  0.6 59.9 %grads_and_sum.1 = (bf16[256,512]{1,0:T(8,128)(2,1)S(1)}, bf16[6,4,1,256,128]{4,3,2,1,0:T(8,128)(2,1)S(1)}, bf16[4,256,512]{2,1,0:T(8,128)(2,1)S(1)}) custom-call(bf16[256,512]{1,0:T(8,128)(2,1)} %q_hbm.1, bf16[256,512]{1,0:T(8,128)(2,1)} %k_hbm.1, bf16[256,512]{1,0:T(8,128)(2,1)} %v_hbm.1, f32[2,256]{1,0:T(2,128)} %r_hbm.1, bf16[2,256,512]{2,1,0:T(8,128)(2,1)} %wg_hbm.1, ...), custom_call_target="tpu_custom_call" | custom-call | tf_op jit(solution)/shard_map/grads_and_sum/pallas_call | solution.py:343
  60.5 5.7 %newton.1 = (bf16[256,512]{1,0:T(8,128)(2,1)}, bf16[2,256,512]{2,1,0:T(8,128)(2,1)}, bf16[2,256,512]{2,1,0:T(8,128)(2,1)}, bf16[2,256,512]{2,1,0:T(8,128)(2,1)}) custom-call(bf16[6,4,1,256,128]{4,3,2,1,0:T(8,128)(2,1)S(1)} %get-tuple-element.7.t_ref, bf16[4,256,512]{2,1,0:T(8,128)(2,1)S(1)} %get-tuple-element.8.begun_ref, ...), custom_call_target="tpu_custom_call" | custom-call | tf_op jit(solution)/shard_map/newton/pallas_call | solution.py:375
